TPU v7x, 32 devices: a whole 2x2x4 slice. The times are simulated.
32 devices in a mesh: leaf: 8 (over z, y), sub: 4 (over x, core).
Axes of the slice: x: 2, y: 2, z: 4, core: 2. Of those that a mesh axis runs over, the one named last changes fastest.
Arguments:
- points: float32 [3, 131072], P(None, ('leaf', 'sub')), may hold values from 0 to 256, as said below
- vectors: float32 [32, 131072], P(None, ('leaf', 'sub')), may hold values from -6 to 6
- counts: int32 [256, 8], P(('leaf', 'sub')), may hold values from 1 to 64, 384 in all within a row
Outputs:
- product: float32 [32, 131072], P(None, ('leaf', 'sub'))
Inputs may be any that keep to these rules, and one draw needn't show every extreme that they name: `points`: rows 0, 1, 2 are x, y, z. The slots of leaf l = 8 s + 4 cz + 2 cy + cx lie in its cell: x in [cx / 2, (cx + 1) / 2], y in [cy / 2, (cy + 1) / 2], z in [s + cz / 2, s + (cz + 1) / 2]. Leaf 8 s + c holds its points in its first counts[s, c] slots; later slots are empty. Each row sums to 384 and holds 64 at least once.
All inputs are finite; a program needn't handle non-finite values.
Results may differ from a plain program's by a relative error of at most 0.0003.
Values sent between devices are 32-bit elements; how exact they have to be, the bound alone decides.
A program may use at most 128 MiB of HBM per device.

v0:
```python
import functools
import math

import jax
import jax.numpy as jnp
import numpy as np
from jax import lax
from jax.experimental import pallas as pl
from jax.experimental.pallas import tpu as pltpu
from jax.sharding import PartitionSpec as P

ORDER = 4


TERM_SCALE = 1.0 / 32.0
ROOT_THREE = math.sqrt(3.0)
far_offsets = (-3, -2, 2, 3)
far_sources = ((0, (0, 4, 5)), (1, (0, 1, 5)))


def term_lengths(slab_count):
    term_count = (slab_count.bit_length() - 1) // 3 + 1
    return [slab_count / 4.0 / 8.0**term_index for term_index in range(term_count)]


def chebyshev(order):
    return np.cos((2.0 * np.arange(order) + 1.0) * np.pi / (2.0 * order))


def lagrange_table(values, node_values):
    columns = []
    for anchor in range(len(node_values)):
        product = values * 0.0 + 1.0
        for against in range(len(node_values)):
            if against != anchor:
                product = (
                    product
                    * (values - node_values[against])
                    / (node_values[anchor] - node_values[against])
                )
        columns.append(product)
    return np.stack(columns, -1)


def grid_nodes(node_values):
    number = len(node_values)
    along_z, along_y, along_x = np.meshgrid(
        np.arange(number), np.arange(number), np.arange(number), indexing="ij"
    )
    return np.stack(
        [node_values[along_x.ravel()], node_values[along_y.ravel()], node_values[along_z.ravel()]],
        -1,
    )


def kernel_table(targets, sources, lengths):
    offsets_xyz = targets[:, None, :] - sources[None, :, :]
    distance = np.sqrt(np.sum(offsets_xyz * offsets_xyz, -1))
    summed_terms = distance * 0.0
    for length in lengths:
        scaled = distance * (ROOT_THREE / length)
        summed_terms = summed_terms + TERM_SCALE / math.sqrt(length) * (1.0 + scaled) * np.exp(
            -scaled
        )
    return summed_terms


def child_tables(node_values):
    halves = [
        lagrange_table(side_offset + 0.5 * node_values, node_values) for side_offset in (-0.5, 0.5)
    ]
    identity = np.eye(len(node_values))
    octant_rows = []
    for depth_index in range(2):
        for row_index in range(2):
            for column_index in range(2):
                octant_rows.append(
                    np.kron(np.kron(halves[depth_index], halves[row_index]), halves[column_index])
                )
    octant_array = np.stack(octant_rows).reshape((2, 2, 2) + octant_rows[0].shape)
    half_array = np.stack(
        [np.kron(np.kron(halves[half_index], identity), identity) for half_index in range(2)]
    )
    return (octant_array, half_array)


def leaf_coupling(node_values, depth_index, layer_index, lengths):
    scaled = grid_nodes(node_values) * 0.25
    targets = []
    sources = []
    for row_index in range(2):
        for column_index in range(2):
            targets.append(
                scaled
                + np.array(
                    [(column_index + 0.5) * 0.5, (row_index + 0.5) * 0.5, (depth_index + 0.5) * 0.5]
                )
            )
            sources.append(
                scaled
                + np.array(
                    [(column_index + 0.5) * 0.5, (row_index + 0.5) * 0.5, (layer_index - 1.5) * 0.5]
                )
            )
    return kernel_table(np.concatenate(targets), np.concatenate(sources), lengths)


def coarse_couplings(node_values, height, lengths):
    span = float(1 << height)
    targets = grid_nodes(node_values) * np.array([0.5, 0.5, 0.5 * span])
    return np.stack(
        [
            kernel_table(targets, targets + np.array([0.0, 0.0, offset * span]), lengths)
            for offset in far_offsets
        ]
    )


def halves_bf16(value):
    high = value.astype(jnp.bfloat16)
    low = (value - high.astype(jnp.float32)).astype(jnp.bfloat16)
    return high, low


def np_halves(table):
    table = np.asarray(table, np.float32)
    high = table.astype(jnp.bfloat16)
    low = (table - high.astype(np.float32)).astype(jnp.bfloat16)
    return np.stack([high, low])


def dot3(value, high, low):
    first, second = halves_bf16(value)
    return (
        jnp.dot(first, high, preferred_element_type=jnp.float32)
        + jnp.dot(second, high, preferred_element_type=jnp.float32)
        + jnp.dot(first, low, preferred_element_type=jnp.float32)
    )


def poly_table(node_values):
    number = len(node_values)
    rows = number * number
    table = np.zeros((2, number, 2, rows, 128), np.float32)
    for row in range(rows):
        for which, anchor in enumerate((row % number, row // number)):
            for against in range(number):
                if against == anchor:
                    table[which, against, 1, row] = 1.0
                else:
                    factor = 1.0 / (node_values[anchor] - node_values[against])
                    table[which, against, 0, row] = factor
                    table[which, against, 1, row] = -node_values[against] * factor
    return table


def make_tables(node_values, level_count, lengths):
    octants, halves = child_tables(node_values)
    rank = ORDER**3
    eight = octants.reshape(8, rank, rank)
    leaf_up = np.zeros((2, 8, rank, 2, rank))
    for parity in range(2):
        leaf_up[parity, :, :, parity, :] = eight
    leaf_up = leaf_up.reshape(16 * rank, 2 * rank)
    leaf_down = leaf_up.T
    box_up = np.zeros((2, 2, rank, 2, rank))
    for parity in range(2):
        box_up[parity, :, :, parity, :] = halves
    box_up = box_up.reshape(2, 2 * rank, 2 * rank)
    box_down = np.swapaxes(box_up, 1, 2)
    far = np.zeros((level_count, 2, 2, rank, 2, rank))
    for height in range(level_count):
        m3, m2, p2, p3 = [c.T for c in coarse_couplings(node_values, height, lengths)]
        far[height, 0, 0, :, 0] = m2
        far[height, 0, 0, :, 1] = m3
        far[height, 0, 1, :, 1] = m2
        far[height, 1, 0, :, 0] = p2
        far[height, 1, 1, :, 0] = p3
        far[height, 1, 1, :, 1] = p2
    far = far.reshape(level_count, 2, 2 * rank, 2 * rank)
    leaf_far = np.stack(
        [
            np.concatenate(
                [leaf_coupling(node_values, depth, layer, lengths).T for layer in layers]
            )
            for depth, layers in far_sources
        ]
    )
    return leaf_up, leaf_down, box_up, box_down, far, leaf_far


def kernel_body(
    dims, lengths, pts, vec, cnt, poly, leaf_up, box_up, down_hbm, box_down, far_hbm, leaf_far_hbm,
    out, mw, pw, bd, lc, r2s, kh, kl, acc, send, recv, gsend, gath, low_pairs, ups, locs, ll,
    leaf_down, far, leaf_far, send_sems, recv_sems, gsend_sems, grecv_sems, table_sems,
):
    nleaf, nsub, cubes, levels = dims
    n = nleaf * nsub
    layers = 2 * cubes
    cube_levels = cubes.bit_length() - 1
    nodes = chebyshev(ORDER)
    me = lax.axis_index("leaf") * nsub + lax.axis_index("sub")
    mesh_id = pl.DeviceIdType.MESH

    def place(d):
        return (d // nsub, lax.rem(d, nsub))

    barrier = pltpu.get_barrier_semaphore()

    def greet(k, carry):
        pl.semaphore_signal(
            barrier, inc=1, device_id=place(lax.rem(me + k, n)), device_id_type=mesh_id
        )
        return carry

    lax.fori_loop(1, n, greet, 0)
    table_copies = [
        pltpu.make_async_copy(down_hbm, leaf_down, table_sems.at[0]),
        pltpu.make_async_copy(far_hbm, far, table_sems.at[1]),
        pltpu.make_async_copy(leaf_far_hbm, leaf_far, table_sems.at[2]),
    ]
    for copy in table_copies:
        copy.start()

    first_slab = (me * cubes).astype(jnp.float32)
    lane = lax.broadcasted_iota(jnp.int32, (1, 256), 1)
    quarter = lane // 64
    slot = lane - quarter * 64
    centre_x = ((quarter % 2).astype(jnp.float32) + 0.5) * 0.5
    centre_y = ((quarter // 2).astype(jnp.float32) + 0.5) * 0.5
    row8 = lax.broadcasted_iota(jnp.int32, (8, 512), 0)

    def span(z, width=256):
        return pl.ds(pl.multiple_of(z * 256, 256), width)

    def occupancy(z):
        cube, base = z // 2, lax.rem(z, 2) * 4
        limit = jnp.where(
            quarter < 2,
            jnp.where(quarter == 0, cnt[cube, base], cnt[cube, base + 1]),
            jnp.where(quarter == 2, cnt[cube, base + 2], cnt[cube, base + 3]),
        )
        return jnp.where(slot < limit, 1.0, 0.0)

    def poly_of(u, which, rows):
        product = None
        for against in range(ORDER):
            a = poly[which, against, 0, :rows]
            b = poly[which, against, 1, :rows]
            a = jnp.concatenate([a, a], 1)
            b = jnp.concatenate([b, b], 1)
            factor = u * a + b
            product = factor if product is None else product * factor
        return product

    nt = (((1,), (1,)), ((), ()))
    nothing = jnp.zeros((64, 128), jnp.bfloat16)

    def up_layer(z, carry):
        masked = vec[:, span(z)] * occupancy(z)
        mh, ml = halves_bf16(masked)
        mw[0:32, span(z + 1)] = mh
        mw[32:64, span(z + 1)] = ml
        coords = pts[:, span(z)]
        pw[0:3, span(z + 1)] = coords
        depth = (lax.rem(z, 2).astype(jnp.float32) + 0.5) * 0.5
        slab = first_slab + (z // 2).astype(jnp.float32)
        ux = (coords[0:1] - centre_x) * 4.0
        uy = (coords[1:2] - centre_y) * 4.0
        uz = ((coords[2:3] - slab) - depth) * 4.0
        plane = poly_of(ux, 0, 16) * poly_of(uy, 1, 16)
        height = poly_of(uz, 0, 8)
        basis = jnp.concatenate([plane * height[a : a + 1] for a in range(ORDER)], 0)
        high = basis.astype(jnp.bfloat16).astype(jnp.float32)
        low = basis - high
        for leaf in range(4):
            start = leaf // 2 * 128
            mine = (quarter == leaf)[:, start : start + 128]
            for which, part in ((0, high), (1, low)):
                own = jnp.where(mine, part[:, start : start + 128], 0.0).astype(jnp.bfloat16)
                both = [own, nothing] if leaf < 2 else [nothing, own]
                bd[which, z, leaf * 64 : leaf * 64 + 64] = jnp.concatenate(both, 1)
        both = lax.dot_general(
            jnp.concatenate([mh, ml], 0), bd[0, z], nt, preferred_element_type=jnp.float32
        )
        rest = lax.dot_general(mh, bd[1, z], nt, preferred_element_type=jnp.float32)
        lc[z + 2] = both[0:32] + both[32:64] + rest
        return carry

    lax.fori_loop(0, layers, up_layer, 0, unroll=2)

    pairs = cubes // 2
    lane128 = lax.broadcasted_iota(jnp.int32, (16, 128), 1)
    offsets = []
    base = 128 + 32 * cube_levels

    def rise():
        own = lc[2 : 2 + layers].reshape(pairs, 4, 32, 256)
        flat = jnp.concatenate([own[:, i].reshape(pairs * 32, 256) for i in range(4)], 1)
        level = dot3(flat, leaf_up[0], leaf_up[1]).reshape(pairs, 32, 128)
        yield
        offset = 0
        for height in range(cube_levels):
            offsets.append(offset)
            count = pairs >> height
            low_pairs[offset + 1 : offset + 1 + count] = level
            send[0, 128 + 32 * height : 160 + 32 * height] = level[0]
            send[1, 128 + 32 * height : 160 + 32 * height] = level[count - 1]
            offset += count + 2
            if count > 1:
                two = level.reshape(count // 2, 2, 32, 128)
                level = dot3(
                    two[:, 0].reshape(count * 16, 128), box_up[0, 0], box_up[1, 0]
                ) + dot3(two[:, 1].reshape(count * 16, 128), box_up[0, 1], box_up[1, 1])
                level = level.reshape(count // 2, 32, 128)
                yield
        box = dot3(level[0], box_up[0, 0], box_up[1, 0])
        folded = jnp.where(lane128 < 64, box[0:16], pltpu.roll(box[16:32], 64, 1))
        gsend[...] = folded
        gath[me] = folded
        yield
        for side, edge in ((0, 0), (1, layers - 1)):
            masked = vec[:, edge * 256 : edge * 256 + 256] * occupancy(jnp.int32(edge))
            coords = pts[:, edge * 256 : edge * 256 + 256]
            for half in range(2):
                cols = slice(half * 128, half * 128 + 128)
                send[side, base + 32 * half : base + 32 + 32 * half] = masked[:, cols]
                send[side, base + 64 + 8 * half : base + 67 + 8 * half] = coords[:, cols]
                for i in range(2):
                    source = lc[2 + i] if side == 0 else lc[layers + i]
                    start = (2 * i + half) * 32
                    send[side, start : start + 32] = source[:, cols]
        pad = jnp.zeros((5, 128), jnp.float32)
        for side in range(2):
            for half in range(2):
                send[side, base + 67 + 8 * half : base + 72 + 8 * half] = pad

    def near_squared(z, p, with_self=True):
        boundary = first_slab + (z + 1).astype(jnp.float32) * 0.5
        block = pw[:, span(z + 1, 512)]
        x = block[0:1] - 0.5
        y = block[1:2] - 0.5
        d = block[2:3] - boundary
        norm = x * x + y * y + d * d
        one = jnp.where(row8 == 4, 1.0, 0.0)
        right = jnp.where(row8 == 0, x, jnp.where(row8 == 1, y, jnp.where(row8 == 2, d,
            jnp.where(row8 == 3, norm, one))))
        swap = jnp.where(row8 == 3, 1.0, jnp.where(row8 == 4, norm, 0.0))
        left = jnp.where(row8 < 3, -2.0 * right, swap)[:, 0:256]

        def thirds(v):
            h = v.astype(jnp.bfloat16).astype(jnp.float32)
            m = (v - h).astype(jnp.bfloat16).astype(jnp.float32)
            return h, m, v - h - m

        rh, rm, rl = thirds(right)
        lh, lm, lo = thirds(left)
        if not with_self:
            rh, rm, rl = rh[:, 256:], rm[:, 256:], rl[:, 256:]
        rs = jnp.concatenate([rh, rm, rh, rl, rm, rh], 0).astype(jnp.bfloat16)
        ls = jnp.concatenate([lh, lh, lm, lh, lm, lo], 0).astype(jnp.bfloat16)
        r2s[p, :, (0 if with_self else 256) : 512] = lax.dot_general(
            ls, rs, (((0,), (0,)), ((), ())), preferred_element_type=jnp.float32
        )

    def near_kernel(p, with_self=True, filler=None, every=4):
        for chunk in range(16):
            if filler is not None and chunk % every == 0:
                next(filler, None)
            rows = slice(chunk * 16, chunk * 16 + 16)
            c0 = (0 if chunk < 8 else 128) if with_self else 256
            sq = jnp.maximum(r2s[p, rows, c0:512], 1e-20)
            r = sq * lax.rsqrt(sq)
            total = None
            for length in lengths:
                rate = ROOT_THREE / length
                weight = TERM_SCALE / math.sqrt(length)
                term = (weight + (weight * rate) * r) * jnp.exp2(r * (-rate * math.log2(math.e)))
                total = term if total is None else total + term
            high = total.astype(jnp.bfloat16)
            kh[p, rows, c0:512] = high
            kl[p, rows, c0:512] = (total - high.astype(jnp.float32)).astype(jnp.bfloat16)

    def plain(m, rows, cols, p):
        both = jnp.dot(m, kh[p, rows, cols], preferred_element_type=jnp.float32)
        rest = jnp.dot(m[0:32], kl[p, rows, cols], preferred_element_type=jnp.float32)
        return both[0:32] + both[32:64] + rest

    def turned(m, rows, cols, p):
        both = lax.dot_general(m, kh[p, rows, cols], nt, preferred_element_type=jnp.float32)
        rest = lax.dot_general(m[0:32], kl[p, rows, cols], nt, preferred_element_type=jnp.float32)
        return both[0:32] + both[32:64] + rest

    first, second, whole = slice(0, 128), slice(128, 256), slice(0, 256)

    def near_apply(z, p):
        here = mw[:, span(z + 1)]
        there = mw[:, span(z + 2)]
        top = plain(here[:, first], first, slice(0, 512), p)
        low = plain(here[:, second], second, slice(128, 512), p)
        back_first = turned(
            jnp.concatenate([here[:, second], there], 1), first, slice(128, 512), p
        )
        back_second = turned(there, second, slice(256, 512), p)
        a0 = top[:, 0:128] + back_first
        a1 = top[:, 128:256] + low[:, 0:128] + back_second
        acc[:, span(z + 1)] += jnp.concatenate([a0, a1], 1)
        acc[:, span(z + 2)] = top[:, 256:512] + low[:, 128:384]

    def near_step(z, p, filler=None, every=4):
        near_squared(z + 1, 1 - p)
        near_kernel(p, True, filler, every)
        near_apply(z - 1, 1 - p)

    def near_four(t, carry):
        for i in range(4):
            near_step(4 * t + (i + 1), (i + 1) % 2)
        return carry

    acc[:, 256:512] = jnp.zeros((32, 256), jnp.float32)
    late = layers // 4 - 1
    rising = rise()
    near_squared(jnp.int32(0), 0)
    next(rising)
    near_squared(jnp.int32(1), 1)
    near_kernel(0, True, rising, 5)
    for z in range(1, 5):
        near_step(jnp.int32(z), z % 2, rising, 5)
    for _ in rising:
        pass

    @pl.when(me == 0)
    def _():
        recv[0] = jnp.zeros(recv.shape[1:], jnp.float32)

    @pl.when(me == n - 1)
    def _():
        recv[1] = jnp.zeros(recv.shape[1:], jnp.float32)

    pl.semaphore_wait(barrier, n - 1)
    to_left = pltpu.make_async_remote_copy(
        send.at[0], recv.at[1], send_sems.at[0], recv_sems.at[1],
        device_id=place(lax.rem(me + n - 1, n)), device_id_type=mesh_id,
    )
    to_right = pltpu.make_async_remote_copy(
        send.at[1], recv.at[0], send_sems.at[1], recv_sems.at[0],
        device_id=place(lax.rem(me + 1, n)), device_id_type=mesh_id,
    )

    @pl.when(me > 0)
    def _():
        to_left.start()

    @pl.when(me < n - 1)
    def _():
        to_right.start()

    def spread(k, target):
        return pltpu.make_async_remote_copy(
            gsend, gath.at[me], gsend_sems.at[k], grecv_sems.at[me],
            device_id=place(target), device_id_type=mesh_id,
        )

    def spread_start(k, carry):
        spread(k, lax.rem(me + k, n)).start()
        return carry

    lax.fori_loop(1, n, spread_start, 0)

    lax.fori_loop(1, late, near_four, 0)

    @pl.when(me > 0)
    def _():
        to_right.wait_recv()

    @pl.when(me < n - 1)
    def _():
        to_left.wait_recv()

    for side, window in ((0, 0), (1, layers + 1)):
        for half in range(2):
            cols = slice(window * 256 + half * 128, window * 256 + half * 128 + 128)
            masked = recv[side, base + 32 * half : base + 32 + 32 * half]
            mh, ml = halves_bf16(masked)
            mw[0:32, cols] = mh
            mw[32:64, cols] = ml
            pw[:, cols] = recv[side, base + 64 + 8 * half : base + 72 + 8 * half]
        for i in range(2):
            at = i if side == 0 else layers + 2 + i
            for half in range(2):
                start = (2 * i + half) * 32
                lc[at, :, half * 128 : half * 128 + 128] = recv[side, start : start + 32]
        for height in range(cube_levels):
            at = offsets[height] + (0 if side == 0 else (pairs >> height) + 1)
            low_pairs[at] = recv[side, 128 + 32 * height : 160 + 32 * height]
    low_far = []

    def leaves():
        window = lc[...].reshape(cubes + 2, 2, 32, 256)
        for depth, sources in far_sources:
            gathered = jnp.concatenate(
                [window[s // 2 : s // 2 + cubes, s % 2].reshape(cubes * 32, 256) for s in sources], 1
            )
            far_part = dot3(gathered, leaf_far[0, depth], leaf_far[1, depth])
            for j in range(cubes):
                ll[2 * j + depth] = far_part[32 * j : 32 * j + 32]
            yield
        for height in range(cube_levels):
            count = pairs >> height
            at = offsets[height]
            below = low_pairs[at : at + count].reshape(count * 32, 128)
            above = low_pairs[at + 2 : at + 2 + count].reshape(count * 32, 128)
            low_far.append(
                dot3(below, far[0, height, 0], far[1, height, 0])
                + dot3(above, far[0, height, 1], far[1, height, 1])
            )
            yield

    def descend():
        count = n // 2
        blank = jnp.zeros((32, 128), jnp.float32)
        offset = 0
        tops = []
        for height in range(cube_levels, levels):
            tops.append(offset)
            ups[offset] = blank
            ups[offset + count + 1] = blank
            if height == cube_levels:

                folds = gath[...].reshape(count, 2, 16, 128)
                even, odd = folds[:, 0], folds[:, 1]
                near_half = lax.broadcasted_iota(jnp.int32, even.shape, 2) < 64
                ups[1 : 1 + count, 0:16] = jnp.where(near_half, even, pltpu.roll(odd, 64, 2))
                ups[1 : 1 + count, 16:32] = jnp.where(near_half, pltpu.roll(even, 64, 2), odd)
            else:
                two = ups[tops[-2] + 1 : tops[-2] + 1 + 2 * count].reshape(count, 2, 32, 128)
                level = dot3(
                    two[:, 0].reshape(count * 32, 128), box_up[0, 0], box_up[1, 0]
                ) + dot3(two[:, 1].reshape(count * 32, 128), box_up[0, 1], box_up[1, 1])
                ups[offset + 1 : offset + 1 + count] = level.reshape(count, 32, 128)
            offset += count + 2
            count //= 2
            yield

        expansion = None
        for height in range(levels - 1, cube_levels - 1, -1):
            j = me >> (height - cube_levels + 1)
            at = tops[height - cube_levels]
            below, above = ups[at + j], ups[at + j + 2]
            here = dot3(below, far[0, height, 0], far[1, height, 0]) + dot3(
                above, far[0, height, 1], far[1, height, 1]
            )
            if expansion is not None:
                parity = lax.rem(j, 2)
                here = here + dot3(expansion, box_down[0, parity], box_down[1, parity])
            expansion = here
            yield
        for height in range(cube_levels - 1, -1, -1):
            count = pairs >> height
            here = low_far[height]
            if height == cube_levels - 1:
                parity = lax.rem(me, 2)
                expansion = here + dot3(expansion, box_down[0, parity], box_down[1, parity])
            else:
                lower = dot3(expansion, box_down[0, 0], box_down[1, 0]).reshape(count // 2, 1, 32, 128)
                upper = dot3(expansion, box_down[0, 1], box_down[1, 1]).reshape(count // 2, 1, 32, 128)
                expansion = here + jnp.concatenate([lower, upper], 1).reshape(count * 32, 128)
            yield
        yield
        inherited = dot3(expansion, leaf_down[0], leaf_down[1])
        for i in range(4):
            for j in range(pairs):
                ll[4 * j + i] += inherited[32 * j : 32 * j + 32, 256 * i : 256 * i + 256]

    for copy in table_copies:
        copy.wait()
    spreading = leaves()
    near_step(jnp.int32(layers - 3), 1, spreading, 4)
    for _ in spreading:
        pass

    def gather_wait(k, carry):
        source = lax.rem(me + n - k, n)
        pltpu.make_async_remote_copy(
            gsend, gath.at[source], gsend_sems.at[k], grecv_sems.at[source],
            device_id=place(source), device_id_type=mesh_id,
        ).wait_recv()
        return carry

    lax.fori_loop(1, n, gather_wait, 0)

    falling = descend()
    near_step(jnp.int32(layers - 2), 0, falling, 4)
    near_squared(jnp.int32(-1), 0, False)
    near_kernel(1, True, falling, 4)
    near_apply(jnp.int32(layers - 2), 0)
    near_kernel(0, False, falling, 4)
    near_apply(jnp.int32(layers - 1), 1)
    acc[:, 256:512] += plain(mw[:, 0:256], whole, slice(256, 512), 0)
    for _ in falling:
        pass

    def finish(z, carry):
        lh, lo = halves_bf16(ll[z])
        both = jnp.dot(
            jnp.concatenate([lh, lo], 0), bd[0, z], preferred_element_type=jnp.float32
        )
        rest = jnp.dot(lh, bd[1, z], preferred_element_type=jnp.float32)
        value = acc[:, span(z + 1)] + (both[0:32] + both[32:64] + rest)
        out[:, span(z)] = value * occupancy(z)
        return carry

    lax.fori_loop(0, layers, finish, 0, unroll=4)

    @pl.when(me > 0)
    def _():
        to_left.wait_send()

    @pl.when(me < n - 1)
    def _():
        to_right.wait_send()

    def send_wait(k, carry):
        spread(k, lax.rem(me + k, n)).wait_send()
        return carry

    lax.fori_loop(1, n, send_wait, 0)


def local(points, vectors, counts):
    cubes = counts.shape[0]
    nleaf, nsub = lax.axis_size("leaf"), lax.axis_size("sub")
    n = nleaf * nsub
    slab_count = cubes * n
    level_count = slab_count.bit_length() - 2
    cube_levels = cubes.bit_length() - 1
    lengths = term_lengths(slab_count)
    node_values = chebyshev(ORDER)
    leaf_up, leaf_down, box_up, box_down, far, leaf_far = [
        jnp.asarray(np_halves(t)) for t in make_tables(node_values, level_count, lengths)
    ]
    poly = jnp.asarray(poly_table(node_values))
    layers = 2 * cubes
    pairs = cubes // 2
    low_count = sum((pairs >> h) + 2 for h in range(cube_levels))
    top_count = sum((n // 2 >> h) + 2 for h in range(level_count - cube_levels))
    halo_rows = 128 + 32 * cube_levels + 80
    f32, bf16 = jnp.float32, jnp.bfloat16
    vmem = pl.BlockSpec(memory_space=pltpu.VMEM)
    anywhere = pl.BlockSpec(memory_space=pl.ANY)
    return pl.pallas_call(
        functools.partial(kernel_body, (nleaf, nsub, cubes, level_count), lengths),
        out_shape=jax.ShapeDtypeStruct(vectors.shape, f32),
        in_specs=[vmem, vmem, pl.BlockSpec(memory_space=pltpu.SMEM), vmem, vmem, vmem,
                  anywhere, vmem, anywhere, anywhere],
        out_specs=vmem,
        scratch_shapes=[
            pltpu.VMEM((64, (layers + 2) * 256), bf16),
            pltpu.VMEM((8, (layers + 2) * 256), f32),
            pltpu.VMEM((2, layers, 256, 256), bf16),
            pltpu.VMEM((layers + 4, 32, 256), f32),
            pltpu.VMEM((2, 256, 512), f32),
            pltpu.VMEM((2, 256, 512), bf16),
            pltpu.VMEM((2, 256, 512), bf16),
            pltpu.VMEM((32, (layers + 2) * 256), f32),
            pltpu.VMEM((2, halo_rows, 128), f32),
            pltpu.VMEM((2, halo_rows, 128), f32),
            pltpu.VMEM((16, 128), f32),
            pltpu.VMEM((n, 16, 128), f32),
            pltpu.VMEM((low_count, 32, 128), f32),
            pltpu.VMEM((top_count, 32, 128), f32),
            pltpu.VMEM((8, 128), f32),
            pltpu.VMEM((layers, 32, 256), f32),
            pltpu.VMEM(leaf_down.shape, bf16),
            pltpu.VMEM(far.shape, bf16),
            pltpu.VMEM(leaf_far.shape, bf16),
            pltpu.SemaphoreType.DMA((2,)),
            pltpu.SemaphoreType.DMA((2,)),
            pltpu.SemaphoreType.DMA((n,)),
            pltpu.SemaphoreType.DMA((n,)),
            pltpu.SemaphoreType.DMA((3,)),
        ],
        compiler_params=pltpu.CompilerParams(
            collective_id=0, has_side_effects=True, vmem_limit_bytes=60 * 1024 * 1024
        ),
    )(points, vectors, counts, poly, leaf_up, box_up, leaf_down, box_down, far, leaf_far)


def solution(mesh):
    in_specs = (P(None, ("leaf", "sub")), P(None, ("leaf", "sub")), P(("leaf", "sub"), None))
    out_specs = P(None, ("leaf", "sub"))
    return jax.shard_map(local, mesh=mesh, in_specs=in_specs, out_specs=out_specs, check_vma=False)
```

profile of v0, /device:TPU:1, one launch (start us, length us, event | category | flops | bytes accessed | tf_op | source)
XLA Modules:
  0.0 25.4 jit_solution(3254658189359654841)
XLA Ops:
  0.0 23.5 %shard_map.100 = f32[32,4096]{1,0:T(8,128)} custom-call(f32[3,4096]{1,0:T(4,128)} %pts.1, f32[32,4096]{1,0:T(8,128)} %vec.1, s32[8,8]{1,0:T(8,128)} %cnt.1, f32[2,4,2,16,128]{4,3,2,1,0:T(8,128)} %constant.20.clone.poly, bf16[2,1024,128]{2,1,0:T(8,128)(2,1)} %constant.14.clone.leaf_up, bf16[2,2,128,128]{3,2,1,0:T(8,128)(2,1)} %constant.16.clone.box_up, ...), custom_call_target="tpu_custom_call" | custom-call | tf_op jit(solution)/shard_map/pallas_call | solution.py:651
  23.5 1.9 %copy.12 = f32[32,4096]{1,0:T(8,128)} copy(f32[32,4096]{1,0:T(8,128)} %shard_map.100) | data formatting | bytes 1048576
where the time goes:
time: 25.6 us; the launch traced here: 25.4 us
  Pallas kernels  23.5 us (92%)
  local copies, waits for them, and re-layouts  1.87 us (7%)
    pallas_call x1, Pallas kernels, local(): pl.pallas_call(functools.partial(kernel_body, (nleaf, nsub, cubes, level_...  23.5 us
    unnamed x1, local copies, waits for them, and re-layouts  1.87 us

commit v1 on v0

--- a/solution.py
+++ b/solution.py
@@ -129,13 +129,60 @@
     return np.stack([high, low])
 
 
+def dot_split(first, second, high, low):
+    return jnp.dot(
+        jnp.concatenate([first, second, first], 1), jnp.concatenate([high, high, low], 0),
+        preferred_element_type=jnp.float32,
+    )
+
+
 def dot3(value, high, low):
-    first, second = halves_bf16(value)
-    return (
-        jnp.dot(first, high, preferred_element_type=jnp.float32)
-        + jnp.dot(second, high, preferred_element_type=jnp.float32)
-        + jnp.dot(first, low, preferred_element_type=jnp.float32)
-    )
+    return dot_split(*halves_bf16(value), high, low)
+
+
+def smooth_split(lengths):
+    r = np.linspace(0.0, math.sqrt(3.0) * 1.0005, 2001)
+    s = r * r
+
+    def term(length):
+        a = r * (ROOT_THREE / length)
+        return TERM_SCALE / math.sqrt(length) * (1.0 + a) * np.exp(-a)
+
+    smooth = sum(term(length) for length in lengths[:-1])
+    basis = np.stack([np.ones_like(r), s, s * r, s * s], 1)
+    weight = np.ones_like(r)
+    for _ in range(100):
+        root = np.sqrt(weight)
+        fitted = np.linalg.lstsq(basis * root[:, None], smooth * root, rcond=None)[0]
+        error = np.abs(smooth - basis @ fitted)
+        weight = weight * (error / error.max() + 1e-3)
+        weight = weight / weight.mean()
+    full = smooth + term(lengths[-1])
+    low = basis[:, :2]
+    c0, c1 = np.linalg.lstsq(low / full[:, None], np.ones_like(r), rcond=None)[0]
+    return (float(c0), float(c1)), [float(v) for v in fitted - np.array([c0, c1, 0.0, 0.0])]
+
+
+def moment_tables(node_values, c0, c1):
+    nodes = grid_nodes(node_values) * 0.25
+    layer_nodes = []
+    for row_index in range(2):
+        for column_index in range(2):
+            layer_nodes.append(nodes + np.array([0.5 * column_index - 0.25, 0.5 * row_index - 0.25, 0.0]))
+    x, y, d = np.concatenate(layer_nodes).T
+    norm = x * x + y * y + d * d
+    one = np.ones_like(x)
+    gather = np.zeros((len(x), 128))
+    spread = np.zeros((128, len(x)))
+    for group, step in enumerate((-1.0, 0.0, 1.0)):
+        source = (
+            c0 + c1 * (norm + step * step / 4.0 + step * d), -2.0 * c1 * x, -2.0 * c1 * y,
+            -c1 * (2.0 * d + step), c1 * one,
+        )
+        for index, (column, row) in enumerate(zip(source, (one, x, y, d, norm))):
+            gather[:, 8 * group + index] = column
+            spread[8 * group + index] = row
+    return gather, spread
 
 
 def poly_table(node_values):
@@ -190,8 +237,9 @@
 
 
 def kernel_body(
-    dims, lengths, pts, vec, cnt, poly, leaf_up, box_up, down_hbm, box_down, far_hbm, leaf_far_hbm,
-    out, mw, pw, bd, lc, r2s, kh, kl, acc, send, recv, gsend, gath, low_pairs, ups, locs, ll,
+    dims, lengths, pieces, pts, vec, cnt, poly, leaf_up, box_up, down_hbm, box_down, far_hbm,
+    leaf_far_hbm, moment_in, moment_out,
+    out, mw, pw, bd, lc, lh, ls, r2s, kn, acc, send, recv, gsend, gath, low_pairs, ups, locs, ll,
     leaf_down, far, leaf_far, send_sems, recv_sems, gsend_sems, grecv_sems, table_sems,
 ):
     nleaf, nsub, cubes, levels = dims
@@ -259,8 +307,7 @@
     def up_layer(z, carry):
         masked = vec[:, span(z)] * occupancy(z)
         mh, ml = halves_bf16(masked)
-        mw[0:32, span(z + 1)] = mh
-        mw[32:64, span(z + 1)] = ml
+        mw[:, span(z + 1)] = mh
         coords = pts[:, span(z)]
         pw[0:3, span(z + 1)] = coords
         depth = (lax.rem(z, 2).astype(jnp.float32) + 0.5) * 0.5
@@ -284,7 +331,9 @@
             jnp.concatenate([mh, ml], 0), bd[0, z], nt, preferred_element_type=jnp.float32
         )
         rest = lax.dot_general(mh, bd[1, z], nt, preferred_element_type=jnp.float32)
-        lc[z + 2] = both[0:32] + both[32:64] + rest
+        coeffs = both[0:32] + both[32:64] + rest
+        lc[z + 2] = coeffs
+        lh[z + 2], ls[z + 2] = halves_bf16(coeffs)
         return carry
 
     lax.fori_loop(0, layers, up_layer, 0, unroll=2)
@@ -295,9 +344,11 @@
     base = 128 + 32 * cube_levels
 
     def rise():
-        own = lc[2 : 2 + layers].reshape(pairs, 4, 32, 256)
-        flat = jnp.concatenate([own[:, i].reshape(pairs * 32, 256) for i in range(4)], 1)
-        level = dot3(flat, leaf_up[0], leaf_up[1]).reshape(pairs, 32, 128)
+        flat = []
+        for part in (lh, ls):
+            own = part[2 : 2 + layers].reshape(pairs, 4, 32, 256)
+            flat.append(jnp.concatenate([own[:, i].reshape(pairs * 32, 256) for i in range(4)], 1))
+        level = dot_split(*flat, leaf_up[0], leaf_up[1]).reshape(pairs, 32, 128)
         yield
         offset = 0
         for height in range(cube_levels):
@@ -363,6 +414,10 @@
             ls, rs, (((0,), (0,)), ((), ())), preferred_element_type=jnp.float32
         )
 
+    rate = ROOT_THREE / lengths[-1]
+    weight = TERM_SCALE / math.sqrt(lengths[-1])
+    d0, d1, q0, q1 = pieces
+
     def near_kernel(p, with_self=True, filler=None, every=4):
         for chunk in range(16):
             if filler is not None and chunk % every == 0:
@@ -371,41 +426,27 @@
             c0 = (0 if chunk < 8 else 128) if with_self else 256
             sq = jnp.maximum(r2s[p, rows, c0:512], 1e-20)
             r = sq * lax.rsqrt(sq)
-            total = None
-            for length in lengths:
-                rate = ROOT_THREE / length
-                weight = TERM_SCALE / math.sqrt(length)
-                term = (weight + (weight * rate) * r) * jnp.exp2(r * (-rate * math.log2(math.e)))
-                total = term if total is None else total + term
-            high = total.astype(jnp.bfloat16)
-            kh[p, rows, c0:512] = high
-            kl[p, rows, c0:512] = (total - high.astype(jnp.float32)).astype(jnp.bfloat16)
+            decay = jnp.exp2(r * (-rate * math.log2(math.e)))
+            rest = d0 + sq * (d1 + r * (q0 + r * q1))
+            kn[p, rows, c0:512] = ((weight + (weight * rate) * r) * decay + rest).astype(jnp.bfloat16)
+
+    first, second, whole = slice(0, 128), slice(128, 256), slice(0, 256)
 
     def plain(m, rows, cols, p):
-        both = jnp.dot(m, kh[p, rows, cols], preferred_element_type=jnp.float32)
-        rest = jnp.dot(m[0:32], kl[p, rows, cols], preferred_element_type=jnp.float32)
-        return both[0:32] + both[32:64] + rest
+        return jnp.dot(m, kn[p, rows, cols], preferred_element_type=jnp.float32)
 
     def turned(m, rows, cols, p):
-        both = lax.dot_general(m, kh[p, rows, cols], nt, preferred_element_type=jnp.float32)
-        rest = lax.dot_general(m[0:32], kl[p, rows, cols], nt, preferred_element_type=jnp.float32)
-        return both[0:32] + both[32:64] + rest
-
-    first, second, whole = slice(0, 128), slice(128, 256), slice(0, 256)
+        return lax.dot_general(m, kn[p, rows, cols], nt, preferred_element_type=jnp.float32)
 
     def near_apply(z, p):
         here = mw[:, span(z + 1)]
         there = mw[:, span(z + 2)]
-        top = plain(here[:, first], first, slice(0, 512), p)
-        low = plain(here[:, second], second, slice(128, 512), p)
-        back_first = turned(
-            jnp.concatenate([here[:, second], there], 1), first, slice(128, 512), p
-        )
-        back_second = turned(there, second, slice(256, 512), p)
-        a0 = top[:, 0:128] + back_first
-        a1 = top[:, 128:256] + low[:, 0:128] + back_second
-        acc[:, span(z + 1)] += jnp.concatenate([a0, a1], 1)
-        acc[:, span(z + 2)] = top[:, 256:512] + low[:, 128:384]
+        own = plain(here[:, first], first, whole, p)
+        low = plain(here[:, second], second, second, p)
+        high = turned(here[:, second], first, second, p)
+        back = turned(there, whole, slice(256, 512), p)
+        acc[:, span(z + 1)] += own + jnp.concatenate([high, low], 1) + back
+        acc[:, span(z + 2)] = plain(here, whole, slice(256, 512), p)
 
     def near_step(z, p, filler=None, every=4):
         near_squared(z + 1, 1 - p)
@@ -481,29 +522,45 @@
         for half in range(2):
             cols = slice(window * 256 + half * 128, window * 256 + half * 128 + 128)
             masked = recv[side, base + 32 * half : base + 32 + 32 * half]
-            mh, ml = halves_bf16(masked)
-            mw[0:32, cols] = mh
-            mw[32:64, cols] = ml
+            mw[:, cols] = masked.astype(jnp.bfloat16)
             pw[:, cols] = recv[side, base + 64 + 8 * half : base + 72 + 8 * half]
         for i in range(2):
             at = i if side == 0 else layers + 2 + i
             for half in range(2):
                 start = (2 * i + half) * 32
-                lc[at, :, half * 128 : half * 128 + 128] = recv[side, start : start + 32]
+                lanes = slice(half * 128, half * 128 + 128)
+                lh[at, :, lanes], ls[at, :, lanes] = halves_bf16(recv[side, start : start + 32])
         for height in range(cube_levels):
             at = offsets[height] + (0 if side == 0 else (pairs >> height) + 1)
             low_pairs[at] = recv[side, 128 + 32 * height : 160 + 32 * height]
     low_far = []
 
     def leaves():
-        window = lc[...].reshape(cubes + 2, 2, 32, 256)
+        spans = slice(1, layers + 3)
+        rows = (layers + 2) * 32
+        moments = dot_split(
+            lh[spans].reshape(rows, 256), ls[spans].reshape(rows, 256), moment_in[0], moment_in[1]
+        ).reshape(layers + 2, 32, 128)
+        lane3 = lax.broadcasted_iota(jnp.int32, (layers, 32, 128), 2)
+        joined = jnp.where(
+            lane3 < 8, moments[0:layers],
+            jnp.where(lane3 < 16, moments[1 : layers + 1], moments[2 : layers + 2]),
+        )
+        ll[...] = dot3(joined.reshape(layers * 32, 128), moment_out[0], moment_out[1]).reshape(
+            layers, 32, 256
+        )
+        yield
+        windows = [part[...].reshape(cubes + 2, 2, 32, 256) for part in (lh, ls)]
         for depth, sources in far_sources:
-            gathered = jnp.concatenate(
-                [window[s // 2 : s // 2 + cubes, s % 2].reshape(cubes * 32, 256) for s in sources], 1
-            )
-            far_part = dot3(gathered, leaf_far[0, depth], leaf_far[1, depth])
+            gathered = [
+                jnp.concatenate(
+                    [w[s // 2 : s // 2 + cubes, s % 2].reshape(cubes * 32, 256) for s in sources], 1
+                )
+                for w in windows
+            ]
+            far_part = dot_split(*gathered, leaf_far[0, depth], leaf_far[1, depth])
             for j in range(cubes):
-                ll[2 * j + depth] = far_part[32 * j : 32 * j + 32]
+                ll[2 * j + depth] += far_part[32 * j : 32 * j + 32]
             yield
         for height in range(cube_levels):
             count = pairs >> height
@@ -640,6 +697,8 @@
         jnp.asarray(np_halves(t)) for t in make_tables(node_values, level_count, lengths)
     ]
     poly = jnp.asarray(poly_table(node_values))
+    (c0, c1), pieces = smooth_split(lengths)
+    moment_in, moment_out = [jnp.asarray(np_halves(t)) for t in moment_tables(node_values, c0, c1)]
     layers = 2 * cubes
     pairs = cubes // 2
     low_count = sum((pairs >> h) + 2 for h in range(cube_levels))
@@ -649,18 +708,19 @@
     vmem = pl.BlockSpec(memory_space=pltpu.VMEM)
     anywhere = pl.BlockSpec(memory_space=pl.ANY)
     return pl.pallas_call(
-        functools.partial(kernel_body, (nleaf, nsub, cubes, level_count), lengths),
+        functools.partial(kernel_body, (nleaf, nsub, cubes, level_count), lengths, pieces),
         out_shape=jax.ShapeDtypeStruct(vectors.shape, f32),
         in_specs=[vmem, vmem, pl.BlockSpec(memory_space=pltpu.SMEM), vmem, vmem, vmem,
-                  anywhere, vmem, anywhere, anywhere],
+                  anywhere, vmem, anywhere, anywhere, vmem, vmem],
         out_specs=vmem,
         scratch_shapes=[
-            pltpu.VMEM((64, (layers + 2) * 256), bf16),
+            pltpu.VMEM((32, (layers + 2) * 256), bf16),
             pltpu.VMEM((8, (layers + 2) * 256), f32),
             pltpu.VMEM((2, layers, 256, 256), bf16),
             pltpu.VMEM((layers + 4, 32, 256), f32),
+            pltpu.VMEM((layers + 4, 32, 256), bf16),
+            pltpu.VMEM((layers + 4, 32, 256), bf16),
             pltpu.VMEM((2, 256, 512), f32),
-            pltpu.VMEM((2, 256, 512), bf16),
             pltpu.VMEM((2, 256, 512), bf16),
             pltpu.VMEM((32, (layers + 2) * 256), f32),
             pltpu.VMEM((2, halo_rows, 128), f32),
@@ -683,7 +743,8 @@
         compiler_params=pltpu.CompilerParams(
             collective_id=0, has_side_effects=True, vmem_limit_bytes=60 * 1024 * 1024
         ),
-    )(points, vectors, counts, poly, leaf_up, box_up, leaf_down, box_down, far, leaf_far)
+    )(points, vectors, counts, poly, leaf_up, box_up, leaf_down, box_down, far, leaf_far,
+      moment_in, moment_out)
 
 
 def solution(mesh):

time: 25.6 us -> 25 us (0.977)
  Pallas kernels: 23.5 us -> 22.9 us
    pallas_call x1, Pallas kernels: 23.5 us -> 22.9 us  [local(): pl.pallas_call(functools.partial(kernel_body, (nleaf, nsub, cubes, level_...]
where the time goes in v1:
time: 25 us; the launch traced here: 24.8 us
  Pallas kernels  22.9 us (92%)
  local copies, waits for them, and re-layouts  1.87 us (7%)
    pallas_call x1, Pallas kernels, local(): pl.pallas_call(functools.partial(kernel_body, (nleaf, nsub, cubes, level_...  22.9 us
    unnamed x1, local copies, waits for them, and re-layouts  1.87 us

profile of v1, /device:TPU:1, one launch (start us, length us, event | category | flops | bytes accessed | tf_op | source)
XLA Modules:
  0.0 24.8 jit_solution(9398135786272467965)
XLA Ops:
  0.0 22.9 %shard_map.118 = f32[32,4096]{1,0:T(8,128)} custom-call(f32[3,4096]{1,0:T(4,128)} %pts.1, f32[32,4096]{1,0:T(8,128)} %vec.1, s32[8,8]{1,0:T(8,128)} %cnt.1, f32[2,4,2,16,128]{4,3,2,1,0:T(8,128)} %constant.24.clone.poly, bf16[2,1024,128]{2,1,0:T(8,128)(2,1)} %constant.18.clone.leaf_up, bf16[2,2,128,128]{3,2,1,0:T(8,128)(2,1)} %constant.20.clone.box_up, ...), custom_call_target="tpu_custom_call" | custom-call | tf_op jit(solution)/shard_map/pallas_call | solution.py:710
  23.0 1.9 %copy.14 = f32[32,4096]{1,0:T(8,128)} copy(f32[32,4096]{1,0:T(8,128)} %shard_map.118) | data formatting | bytes 1048576

commit v2 on v1

--- a/solution.py
+++ b/solution.py
@@ -10,6 +10,8 @@
 from jax.sharding import PartitionSpec as P
 
 ORDER = 4
+SOONER_HOPS = 1
+VMEM_BYTES = 60 * 1024 * 1024
 
 
 TERM_SCALE = 1.0 / 32.0
@@ -185,20 +187,12 @@
     return gather, spread
 
 
-def poly_table(node_values):
-    number = len(node_values)
-    rows = number * number
-    table = np.zeros((2, number, 2, rows, 128), np.float32)
-    for row in range(rows):
-        for which, anchor in enumerate((row % number, row // number)):
-            for against in range(number):
-                if against == anchor:
-                    table[which, against, 1, row] = 1.0
-                else:
-                    factor = 1.0 / (node_values[anchor] - node_values[against])
-                    table[which, against, 0, row] = factor
-                    table[which, against, 1, row] = -node_values[against] * factor
-    return table
+def lagrange_coefficients(node_values):
+    rows = []
+    for anchor in range(len(node_values)):
+        others = np.delete(node_values, anchor)
+        rows.append(np.poly(others)[::-1] / np.prod(node_values[anchor] - others))
+    return np.stack(rows)
 
 
 def make_tables(node_values, level_count, lengths):
@@ -237,10 +231,11 @@
 
 
 def kernel_body(
-    dims, lengths, pieces, pts, vec, cnt, poly, leaf_up, box_up, down_hbm, box_down, far_hbm,
-    leaf_far_hbm, moment_in, moment_out,
-    out, mw, pw, bd, lc, lh, ls, r2s, kn, acc, send, recv, gsend, gath, low_pairs, ups, locs, ll,
-    leaf_down, far, leaf_far, send_sems, recv_sems, gsend_sems, grecv_sems, table_sems,
+    dims, lengths, pieces, pts_hbm, vec_hbm, cnt, leaf_up_hbm, box_up_hbm, leaf_down_hbm,
+    box_down_hbm, far_hbm, leaf_far_hbm, moment_in_hbm, moment_out_hbm,
+    out, pts, vec, mw, pw, bd, b3, lh, ls, r2s, kn, acc, send, recv, send2, recv2, gsend, gath, crossed,
+    low_pairs, ups, locs, ll, leaf_up, box_up, leaf_down, box_down, far, leaf_far, moment_in,
+    moment_out, send_sems, recv_sems, gsend_sems, grecv_sems, swap_sems, table_sems,
 ):
     nleaf, nsub, cubes, levels = dims
     n = nleaf * nsub
@@ -248,27 +243,31 @@
     cube_levels = cubes.bit_length() - 1
     nodes = chebyshev(ORDER)
     me = lax.axis_index("leaf") * nsub + lax.axis_index("sub")
-    mesh_id = pl.DeviceIdType.MESH
+    mesh_id = pl.DeviceIdType.LOGICAL
 
     def place(d):
-        return (d // nsub, lax.rem(d, nsub))
+        return d
+
+    copies = [
+        pltpu.make_async_copy(source, target, table_sems.at[index])
+        for index, (source, target) in enumerate((
+            (pts_hbm, pts), (vec_hbm, vec), (leaf_up_hbm, leaf_up), (box_up_hbm, box_up),
+            (moment_in_hbm, moment_in), (moment_out_hbm, moment_out), (leaf_far_hbm, leaf_far),
+            (far_hbm, far), (box_down_hbm, box_down), (leaf_down_hbm, leaf_down),
+        ))
+    ]
+    for copy in copies:
+        copy.start()
 
     barrier = pltpu.get_barrier_semaphore()
 
     def greet(k, carry):
         pl.semaphore_signal(
-            barrier, inc=1, device_id=place(lax.rem(me + k, n)), device_id_type=mesh_id
+            barrier, inc=1, device_id=place((me + k) & (n - 1)), device_id_type=mesh_id
         )
         return carry
 
     lax.fori_loop(1, n, greet, 0)
-    table_copies = [
-        pltpu.make_async_copy(down_hbm, leaf_down, table_sems.at[0]),
-        pltpu.make_async_copy(far_hbm, far, table_sems.at[1]),
-        pltpu.make_async_copy(leaf_far_hbm, leaf_far, table_sems.at[2]),
-    ]
-    for copy in table_copies:
-        copy.start()
 
     first_slab = (me * cubes).astype(jnp.float32)
     lane = lax.broadcasted_iota(jnp.int32, (1, 256), 1)
@@ -290,60 +289,111 @@
         )
         return jnp.where(slot < limit, 1.0, 0.0)
 
-    def poly_of(u, which, rows):
-        product = None
-        for against in range(ORDER):
-            a = poly[which, against, 0, :rows]
-            b = poly[which, against, 1, :rows]
-            a = jnp.concatenate([a, a], 1)
-            b = jnp.concatenate([b, b], 1)
-            factor = u * a + b
-            product = factor if product is None else product * factor
-        return product
+    table = lagrange_coefficients(nodes)
+    row16 = lax.broadcasted_iota(jnp.int32, (16, 128), 0)
+
+    def spread_rows(anchor):
+        powers = []
+        for power in range(ORDER):
+            c = [float(v) for v in table[:, power]]
+            one = jnp.where(
+                anchor < 2, jnp.where(anchor == 0, c[0], c[1]), jnp.where(anchor == 2, c[2], c[3])
+            )
+            powers.append(jnp.concatenate([one, one], 1))
+        return powers
+
+    along_x = spread_rows(row16 % ORDER)
+    along_y = spread_rows(row16 // ORDER)
+    along_z = [c[0:8] for c in along_x]
+
+    def poly_of(u, powers):
+        p0, p1, p2, p3 = powers
+        return ((p3 * u + p2) * u + p1) * u + p0
+
+    def basis_of(ux, uy, uz):
+        plane = poly_of(ux, along_x) * poly_of(uy, along_y)
+        height = poly_of(uz, along_z)
+        return halves_bf16(
+            jnp.concatenate([plane * height[a : a + 1] for a in range(ORDER)], 0)
+        )
 
     nt = (((1,), (1,)), ((), ()))
+    left64 = lax.broadcasted_iota(jnp.int32, (64, 128), 1) < 64
     nothing = jnp.zeros((64, 128), jnp.bfloat16)
 
-    def up_layer(z, carry):
+    def box_layer(z, carry):
         masked = vec[:, span(z)] * occupancy(z)
-        mh, ml = halves_bf16(masked)
-        mw[:, span(z + 1)] = mh
+        mw[0:32, span(z + 1)], mw[32:64, span(z + 1)] = halves_bf16(masked)
         coords = pts[:, span(z)]
         pw[0:3, span(z + 1)] = coords
+        b3[0:64, span(z)], b3[64:128, span(z)] = basis_of(
+            coords[0:1] * 2.0 - 1.0, coords[1:2] * 2.0 - 1.0,
+            (coords[2:3] - first_slab) * (2.0 / cubes) - 1.0,
+        )
+        return carry
+
+    def leaf_layer(z, carry):
+        coords = pts[:, span(z)]
         depth = (lax.rem(z, 2).astype(jnp.float32) + 0.5) * 0.5
         slab = first_slab + (z // 2).astype(jnp.float32)
-        ux = (coords[0:1] - centre_x) * 4.0
-        uy = (coords[1:2] - centre_y) * 4.0
-        uz = ((coords[2:3] - slab) - depth) * 4.0
-        plane = poly_of(ux, 0, 16) * poly_of(uy, 1, 16)
-        height = poly_of(uz, 0, 8)
-        basis = jnp.concatenate([plane * height[a : a + 1] for a in range(ORDER)], 0)
-        high = basis.astype(jnp.bfloat16).astype(jnp.float32)
-        low = basis - high
-        for leaf in range(4):
-            start = leaf // 2 * 128
-            mine = (quarter == leaf)[:, start : start + 128]
-            for which, part in ((0, high), (1, low)):
-                own = jnp.where(mine, part[:, start : start + 128], 0.0).astype(jnp.bfloat16)
-                both = [own, nothing] if leaf < 2 else [nothing, own]
-                bd[which, z, leaf * 64 : leaf * 64 + 64] = jnp.concatenate(both, 1)
-        both = lax.dot_general(
-            jnp.concatenate([mh, ml], 0), bd[0, z], nt, preferred_element_type=jnp.float32
-        )
-        rest = lax.dot_general(mh, bd[1, z], nt, preferred_element_type=jnp.float32)
-        coeffs = both[0:32] + both[32:64] + rest
-        lc[z + 2] = coeffs
-        lh[z + 2], ls[z + 2] = halves_bf16(coeffs)
+        high, low = basis_of(
+            (coords[0:1] - centre_x) * 4.0, (coords[1:2] - centre_y) * 4.0,
+            ((coords[2:3] - slab) - depth) * 4.0,
+        )
+        for half in range(2):
+            cols = slice(half * 128, half * 128 + 128)
+            for which, part in ((0, high[:, cols]), (1, low[:, cols])):
+                bd[which, z, half] = jnp.concatenate(
+                    [jnp.where(left64, part, nothing), jnp.where(left64, nothing, part)], 0
+                )
         return carry
 
-    lax.fori_loop(0, layers, up_layer, 0, unroll=2)
+    def couple():
+        edge = [0, 1, layers - 2, layers - 1]
+        for index, z in enumerate(edge + list(range(2, layers - 2))):
+            for half in range(2):
+                cols = slice(half * 128, half * 128 + 128)
+                at = slice(256 * (z + 1) + half * 128, 256 * (z + 1) + half * 128 + 128)
+                main = lax.dot_general(
+                    mw[:, at], bd[0, z, half], nt, preferred_element_type=jnp.float32
+                )
+                rest = lax.dot_general(
+                    mw[0:32, at], bd[1, z, half], nt, preferred_element_type=jnp.float32
+                )
+                coeffs = main[0:32] + main[32:64] + rest
+                if z in edge:
+                    side, i = (0, z) if z < 2 else (1, z - layers + 2)
+                    start = (2 * i + half) * 32
+                    send[side, start : start + 32] = coeffs
+                lh[z + 2, :, cols], ls[z + 2, :, cols] = halves_bf16(coeffs)
+            if index % 2:
+                yield
+
+    copies[0].wait()
+    copies[1].wait()
+    lax.fori_loop(0, layers, box_layer, 0, unroll=4)
+    box = lax.dot_general(
+        mw[:, 256 : 256 + layers * 256], b3[...], nt, preferred_element_type=jnp.float32
+    )
 
     pairs = cubes // 2
     lane128 = lax.broadcasted_iota(jnp.int32, (16, 128), 1)
     offsets = []
-    base = 128 + 32 * cube_levels
+    base = 128
+    box = box[0:32] + box[32:64]
+    box = box + pltpu.roll(box, 64, 1)
+    core = lax.rem(me, 2)
+    folded = [
+        jnp.where(lane128[0:8] < 64, box[16 * k : 16 * k + 8], box[16 * k + 8 : 16 * k + 16])
+        for k in range(2)
+    ]
+    gsend[0] = folded[0]
+    gsend[1] = folded[1]
+    gath[me] = jnp.where(core == 0, folded[0], folded[1])
 
     def rise():
+        for copy in copies[2:4]:
+            copy.wait()
         flat = []
         for part in (lh, ls):
             own = part[2 : 2 + layers].reshape(pairs, 4, 32, 256)
@@ -355,8 +405,8 @@
             offsets.append(offset)
             count = pairs >> height
             low_pairs[offset + 1 : offset + 1 + count] = level
-            send[0, 128 + 32 * height : 160 + 32 * height] = level[0]
-            send[1, 128 + 32 * height : 160 + 32 * height] = level[count - 1]
+            send2[0, 32 * height : 32 * height + 32] = level[0]
+            send2[1, 32 * height : 32 * height + 32] = level[count - 1]
             offset += count + 2
             if count > 1:
                 two = level.reshape(count // 2, 2, 32, 128)
@@ -365,26 +415,18 @@
                 ) + dot3(two[:, 1].reshape(count * 16, 128), box_up[0, 1], box_up[1, 1])
                 level = level.reshape(count // 2, 32, 128)
                 yield
-        box = dot3(level[0], box_up[0, 0], box_up[1, 0])
-        folded = jnp.where(lane128 < 64, box[0:16], pltpu.roll(box[16:32], 64, 1))
-        gsend[...] = folded
-        gath[me] = folded
-        yield
-        for side, edge in ((0, 0), (1, layers - 1)):
-            masked = vec[:, edge * 256 : edge * 256 + 256] * occupancy(jnp.int32(edge))
-            coords = pts[:, edge * 256 : edge * 256 + 256]
-            for half in range(2):
-                cols = slice(half * 128, half * 128 + 128)
-                send[side, base + 32 * half : base + 32 + 32 * half] = masked[:, cols]
-                send[side, base + 64 + 8 * half : base + 67 + 8 * half] = coords[:, cols]
-                for i in range(2):
-                    source = lc[2 + i] if side == 0 else lc[layers + i]
-                    start = (2 * i + half) * 32
-                    send[side, start : start + 32] = source[:, cols]
-        pad = jnp.zeros((5, 128), jnp.float32)
-        for side in range(2):
-            for half in range(2):
-                send[side, base + 67 + 8 * half : base + 72 + 8 * half] = pad
+
+    for side, edge in ((0, 0), (1, layers - 1)):
+        masked = vec[:, edge * 256 : edge * 256 + 256] * occupancy(jnp.int32(edge))
+        coords = pts[:, edge * 256 : edge * 256 + 256]
+        for half in range(2):
+            cols = slice(half * 128, half * 128 + 128)
+            send[side, base + 32 * half : base + 32 + 32 * half] = masked[:, cols]
+            send[side, base + 64 + 8 * half : base + 67 + 8 * half] = coords[:, cols]
+    pad = jnp.zeros((5, 128), jnp.float32)
+    for side in range(2):
+        for half in range(2):
+            send[side, base + 67 + 8 * half : base + 72 + 8 * half] = pad
 
     def near_squared(z, p, with_self=True):
         boundary = first_slab + (z + 1).astype(jnp.float32) * 0.5
@@ -439,8 +481,8 @@
         return lax.dot_general(m, kn[p, rows, cols], nt, preferred_element_type=jnp.float32)
 
     def near_apply(z, p):
-        here = mw[:, span(z + 1)]
-        there = mw[:, span(z + 2)]
+        here = mw[0:32, span(z + 1)]
+        there = mw[0:32, span(z + 2)]
         own = plain(here[:, first], first, whole, p)
         low = plain(here[:, second], second, second, p)
         high = turned(here[:, second], first, second, p)
@@ -458,82 +500,122 @@
             near_step(4 * t + (i + 1), (i + 1) % 2)
         return carry
 
-    acc[:, 256:512] = jnp.zeros((32, 256), jnp.float32)
-    late = layers // 4 - 1
-    rising = rise()
-    near_squared(jnp.int32(0), 0)
-    next(rising)
-    near_squared(jnp.int32(1), 1)
-    near_kernel(0, True, rising, 5)
-    for z in range(1, 5):
-        near_step(jnp.int32(z), z % 2, rising, 5)
-    for _ in rising:
-        pass
-
     @pl.when(me == 0)
     def _():
         recv[0] = jnp.zeros(recv.shape[1:], jnp.float32)
+        recv2[0] = jnp.zeros(recv2.shape[1:], jnp.float32)
 
     @pl.when(me == n - 1)
     def _():
         recv[1] = jnp.zeros(recv.shape[1:], jnp.float32)
-
-    pl.semaphore_wait(barrier, n - 1)
-    to_left = pltpu.make_async_remote_copy(
-        send.at[0], recv.at[1], send_sems.at[0], recv_sems.at[1],
-        device_id=place(lax.rem(me + n - 1, n)), device_id_type=mesh_id,
-    )
-    to_right = pltpu.make_async_remote_copy(
-        send.at[1], recv.at[0], send_sems.at[1], recv_sems.at[0],
-        device_id=place(lax.rem(me + 1, n)), device_id_type=mesh_id,
-    )
-
-    @pl.when(me > 0)
-    def _():
-        to_left.start()
-
-    @pl.when(me < n - 1)
-    def _():
-        to_right.start()
+        recv2[1] = jnp.zeros(recv2.shape[1:], jnp.float32)
+
+    def sideways(source, target, rows, first_sem):
+        to_left = pltpu.make_async_remote_copy(
+            source.at[0, rows], target.at[1, rows],
+            send_sems.at[first_sem], recv_sems.at[first_sem + 1],
+            device_id=place((me + n - 1) & (n - 1)), device_id_type=mesh_id,
+        )
+        to_right = pltpu.make_async_remote_copy(
+            source.at[1, rows], target.at[0, rows],
+            send_sems.at[first_sem + 1], recv_sems.at[first_sem],
+            device_id=place((me + 1) & (n - 1)), device_id_type=mesh_id,
+        )
+        return to_left, to_right
+
+    point_edges = sideways(send, recv, pl.ds(base, 80), 0)
+    leaf_edges = sideways(send, recv, pl.ds(0, base), 2)
+    box_edges = sideways(send2, recv2, pl.ds(0, 32 * cube_levels), 4)
+
+    def wait_edges(pair):
+        edges(pair, lambda pair: pair[1].wait_recv(), lambda pair: pair[0].wait_recv())
+
+    def edges(pair, left_action, right_action):
+        @pl.when(me > 0)
+        def _():
+            left_action(pair)
+
+        @pl.when(me < n - 1)
+        def _():
+            right_action(pair)
+
+    def start_edges(pair):
+        edges(pair, lambda pair: pair[0].start(), lambda pair: pair[1].start())
 
     def spread(k, target):
         return pltpu.make_async_remote_copy(
-            gsend, gath.at[me], gsend_sems.at[k], grecv_sems.at[me],
+            gsend.at[target & 1], gath.at[me], gsend_sems.at[0], grecv_sems.at[0],
             device_id=place(target), device_id_type=mesh_id,
         )
 
     def spread_start(k, carry):
-        spread(k, lax.rem(me + k, n)).start()
+        spread(k, (me + k) & (n - 1)).start()
         return carry
 
-    lax.fori_loop(1, n, spread_start, 0)
-
+    def first_sends():
+        pl.semaphore_wait(barrier, n - 1)
+        lax.fori_loop(1, n, spread_start, 0)
+        start_edges(point_edges)
+
+    hops = lax.rem(me // 2, 2) + lax.rem(me // 4, 2) + me // 8
+    sooner = hops <= SOONER_HOPS
+
+    @pl.when(jnp.logical_not(sooner))
+    def _():
+        first_sends()
+
+    lax.fori_loop(0, layers, leaf_layer, 0, unroll=4)
+
+    acc[:, 256:512] = jnp.zeros((32, 256), jnp.float32)
+    late = layers // 4 - 1
+
+    def climb():
+        yield from couple()
+        yield from rise()
+
+    rising = climb()
+    near_squared(jnp.int32(0), 0)
+    near_squared(jnp.int32(1), 1)
+    near_kernel(0, True, rising, 4)
+    near_step(jnp.int32(1), 1, rising, 4)
+
+    @pl.when(sooner)
+    def _():
+        first_sends()
+
+    start_edges(leaf_edges)
+    for z in range(2, 5):
+        near_step(jnp.int32(z), z % 2, rising, 2)
+    for _ in rising:
+        pass
+    start_edges(box_edges)
     lax.fori_loop(1, late, near_four, 0)
 
-    @pl.when(me > 0)
-    def _():
-        to_right.wait_recv()
-
-    @pl.when(me < n - 1)
-    def _():
-        to_left.wait_recv()
-
-    for side, window in ((0, 0), (1, layers + 1)):
-        for half in range(2):
-            cols = slice(window * 256 + half * 128, window * 256 + half * 128 + 128)
-            masked = recv[side, base + 32 * half : base + 32 + 32 * half]
-            mw[:, cols] = masked.astype(jnp.bfloat16)
-            pw[:, cols] = recv[side, base + 64 + 8 * half : base + 72 + 8 * half]
-        for i in range(2):
-            at = i if side == 0 else layers + 2 + i
+    def take_points():
+        wait_edges(point_edges)
+        for side, window in ((0, 0), (1, layers + 1)):
             for half in range(2):
-                start = (2 * i + half) * 32
-                lanes = slice(half * 128, half * 128 + 128)
-                lh[at, :, lanes], ls[at, :, lanes] = halves_bf16(recv[side, start : start + 32])
-        for height in range(cube_levels):
-            at = offsets[height] + (0 if side == 0 else (pairs >> height) + 1)
-            low_pairs[at] = recv[side, 128 + 32 * height : 160 + 32 * height]
-    low_far = []
+                cols = slice(window * 256 + half * 128, window * 256 + half * 128 + 128)
+                masked = recv[side, base + 32 * half : base + 32 + 32 * half]
+                mw[0:32, cols] = masked.astype(jnp.bfloat16)
+                pw[:, cols] = recv[side, base + 64 + 8 * half : base + 72 + 8 * half]
+
+    def take_leaves():
+        wait_edges(leaf_edges)
+        for side in range(2):
+            for i in range(2):
+                at = i if side == 0 else layers + 2 + i
+                for half in range(2):
+                    start = (2 * i + half) * 32
+                    lanes = slice(half * 128, half * 128 + 128)
+                    lh[at, :, lanes], ls[at, :, lanes] = halves_bf16(recv[side, start : start + 32])
+
+    def take_boxes():
+        wait_edges(box_edges)
+        for side in range(2):
+            for height in range(cube_levels):
+                at = offsets[height] + (0 if side == 0 else (pairs >> height) + 1)
+                low_pairs[at] = recv2[side, 32 * height : 32 * height + 32]
 
     def leaves():
         spans = slice(1, layers + 3)
@@ -562,20 +644,43 @@
             for j in range(cubes):
                 ll[2 * j + depth] += far_part[32 * j : 32 * j + 32]
             yield
-        for height in range(cube_levels):
+
+    def lower():
+        expansion = None
+        for height in reversed(range(cube_levels)):
             count = pairs >> height
             at = offsets[height]
             below = low_pairs[at : at + count].reshape(count * 32, 128)
             above = low_pairs[at + 2 : at + 2 + count].reshape(count * 32, 128)
-            low_far.append(
-                dot3(below, far[0, height, 0], far[1, height, 0])
-                + dot3(above, far[0, height, 1], far[1, height, 1])
+            here = dot3(below, far[0, height, 0], far[1, height, 0]) + dot3(
+                above, far[0, height, 1], far[1, height, 1]
             )
+            if expansion is not None:
+                below, above = [
+                    dot3(expansion, box_down[0, side], box_down[1, side]).reshape(
+                        count // 2, 1, 32, 128
+                    )
+                    for side in range(2)
+                ]
+                here = here + jnp.concatenate([below, above], 1).reshape(count * 32, 128)
+            expansion = here
             yield
+        inherited = dot3(expansion, leaf_down[0], leaf_down[1])
+        yield
+        for i in range(4):
+            for j in range(pairs):
+                ll[4 * j + i] += inherited[32 * j : 32 * j + 32, 256 * i : 256 * i + 256]
+        yield
+
+    partner = me + 1 - 2 * core
+    swap = pltpu.make_async_remote_copy(
+        crossed.at[core], crossed.at[core], swap_sems.at[0], swap_sems.at[1],
+        device_id=place(partner), device_id_type=mesh_id,
+    )
 
     def descend():
         count = n // 2
-        blank = jnp.zeros((32, 128), jnp.float32)
+        blank = jnp.zeros((16, 128), jnp.float32)
         offset = 0
         tops = []
         for height in range(cube_levels, levels):
@@ -584,17 +689,17 @@
             ups[offset + count + 1] = blank
             if height == cube_levels:
 
-                folds = gath[...].reshape(count, 2, 16, 128)
+                folds = gath[...].reshape(count, 2, 8, 128)
                 even, odd = folds[:, 0], folds[:, 1]
                 near_half = lax.broadcasted_iota(jnp.int32, even.shape, 2) < 64
-                ups[1 : 1 + count, 0:16] = jnp.where(near_half, even, pltpu.roll(odd, 64, 2))
-                ups[1 : 1 + count, 16:32] = jnp.where(near_half, pltpu.roll(even, 64, 2), odd)
+                ups[1 : 1 + count, 0:8] = jnp.where(near_half, even, pltpu.roll(odd, 64, 2))
+                ups[1 : 1 + count, 8:16] = jnp.where(near_half, pltpu.roll(even, 64, 2), odd)
             else:
-                two = ups[tops[-2] + 1 : tops[-2] + 1 + 2 * count].reshape(count, 2, 32, 128)
+                two = ups[tops[-2] + 1 : tops[-2] + 1 + 2 * count].reshape(count, 2, 16, 128)
                 level = dot3(
-                    two[:, 0].reshape(count * 32, 128), box_up[0, 0], box_up[1, 0]
-                ) + dot3(two[:, 1].reshape(count * 32, 128), box_up[0, 1], box_up[1, 1])
-                ups[offset + 1 : offset + 1 + count] = level.reshape(count, 32, 128)
+                    two[:, 0].reshape(count * 16, 128), box_up[0, 0], box_up[1, 0]
+                ) + dot3(two[:, 1].reshape(count * 16, 128), box_up[0, 1], box_up[1, 1])
+                ups[offset + 1 : offset + 1 + count] = level.reshape(count, 16, 128)
             offset += count + 2
             count //= 2
             yield
@@ -612,76 +717,82 @@
                 here = here + dot3(expansion, box_down[0, parity], box_down[1, parity])
             expansion = here
             yield
-        for height in range(cube_levels - 1, -1, -1):
-            count = pairs >> height
-            here = low_far[height]
-            if height == cube_levels - 1:
-                parity = lax.rem(me, 2)
-                expansion = here + dot3(expansion, box_down[0, parity], box_down[1, parity])
-            else:
-                lower = dot3(expansion, box_down[0, 0], box_down[1, 0]).reshape(count // 2, 1, 32, 128)
-                upper = dot3(expansion, box_down[0, 1], box_down[1, 1]).reshape(count // 2, 1, 32, 128)
-                expansion = here + jnp.concatenate([lower, upper], 1).reshape(count * 32, 128)
-            yield
-        yield
-        inherited = dot3(expansion, leaf_down[0], leaf_down[1])
-        for i in range(4):
-            for j in range(pairs):
-                ll[4 * j + i] += inherited[32 * j : 32 * j + 32, 256 * i : 256 * i + 256]
-
-    for copy in table_copies:
+        crossed[core] = expansion
+
+    def join_halves():
+        swap.wait_recv()
+        both = jnp.concatenate([crossed[0], crossed[1]], 0)
+        wide = lax.broadcasted_iota(jnp.int32, (32, 128), 1) < 64
+        turned_round = pltpu.roll(both, 64, 1)
+        own = jnp.where(wide == (core == 0), both, turned_round)
+        high, low = halves_bf16(own)
+        locs[...] = jnp.concatenate([high, low], 1)
+
+    def settle():
+        for z in range(layers):
+            lhigh, llow = halves_bf16(ll[z])
+            both = jnp.concatenate([lhigh, llow], 0)
+            parts = []
+            for half in range(2):
+                cols = slice(half * 128, half * 128 + 128)
+                main = jnp.dot(both[:, cols], bd[0, z, half], preferred_element_type=jnp.float32)
+                rest = jnp.dot(lhigh[:, cols], bd[1, z, half], preferred_element_type=jnp.float32)
+                parts.append(main[0:32] + main[32:64] + rest)
+            acc[:, 256 * (z + 1) : 256 * (z + 2)] += jnp.concatenate(parts, 1)
+            if z % 2:
+                yield
+
+    for copy in copies[4:]:
         copy.wait()
+    take_leaves()
     spreading = leaves()
     near_step(jnp.int32(layers - 3), 1, spreading, 4)
     for _ in spreading:
         pass
-
-    def gather_wait(k, carry):
-        source = lax.rem(me + n - k, n)
-        pltpu.make_async_remote_copy(
-            gsend, gath.at[source], gsend_sems.at[k], grecv_sems.at[source],
-            device_id=place(source), device_id_type=mesh_id,
-        ).wait_recv()
-        return carry
-
-    lax.fori_loop(1, n, gather_wait, 0)
-
+    take_points()
+    take_boxes()
+    lowering = lower()
+    near_step(jnp.int32(layers - 2), 0, lowering, 2)
+    for _ in lowering:
+        pass
+    near_squared(jnp.int32(-1), 0, False)
+    near_apply(jnp.int32(layers - 2), 0)
+
+    everyone = pltpu.make_async_remote_copy(
+        gath.at[pl.ds(0, n - 1)], gath.at[pl.ds(0, n - 1)], gsend_sems.at[0], grecv_sems.at[0],
+        device_id=place(partner), device_id_type=mesh_id,
+    )
+    everyone.wait_recv()
     falling = descend()
-    near_step(jnp.int32(layers - 2), 0, falling, 4)
-    near_squared(jnp.int32(-1), 0, False)
-    near_kernel(1, True, falling, 4)
-    near_apply(jnp.int32(layers - 2), 0)
-    near_kernel(0, False, falling, 4)
-    near_apply(jnp.int32(layers - 1), 1)
-    acc[:, 256:512] += plain(mw[:, 0:256], whole, slice(256, 512), 0)
+    near_kernel(1, True, falling, 1)
     for _ in falling:
         pass
+    swap.start()
+    settling = settle()
+    near_kernel(0, False, settling, 2)
+    near_apply(jnp.int32(layers - 1), 1)
+    acc[:, 256:512] += plain(mw[0:32, 0:256], whole, slice(256, 512), 0)
+    for _ in settling:
+        pass
+
+    join_halves()
 
     def finish(z, carry):
-        lh, lo = halves_bf16(ll[z])
-        both = jnp.dot(
-            jnp.concatenate([lh, lo], 0), bd[0, z], preferred_element_type=jnp.float32
-        )
-        rest = jnp.dot(lh, bd[1, z], preferred_element_type=jnp.float32)
-        value = acc[:, span(z + 1)] + (both[0:32] + both[32:64] + rest)
+        value = acc[:, span(z + 1)] + jnp.dot(
+            locs[:, 0:192],
+            jnp.concatenate([b3[:, span(z)], b3[0:64, span(z)]], 0),
+            preferred_element_type=jnp.float32,
+        )
         out[:, span(z)] = value * occupancy(z)
         return carry
 
-    lax.fori_loop(0, layers, finish, 0, unroll=4)
-
-    @pl.when(me > 0)
-    def _():
-        to_left.wait_send()
-
-    @pl.when(me < n - 1)
-    def _():
-        to_right.wait_send()
-
-    def send_wait(k, carry):
-        spread(k, lax.rem(me + k, n)).wait_send()
-        return carry
-
-    lax.fori_loop(1, n, send_wait, 0)
+    lax.fori_loop(0, layers, finish, 0, unroll=8)
+
+    swap.wait_send()
+    for pair in (point_edges, leaf_edges, box_edges):
+        edges(pair, lambda pair: pair[0].wait_send(), lambda pair: pair[1].wait_send())
+
+    everyone.wait_send()
 
 
 def local(points, vectors, counts):
@@ -696,55 +807,55 @@
     leaf_up, leaf_down, box_up, box_down, far, leaf_far = [
         jnp.asarray(np_halves(t)) for t in make_tables(node_values, level_count, lengths)
     ]
-    poly = jnp.asarray(poly_table(node_values))
     (c0, c1), pieces = smooth_split(lengths)
     moment_in, moment_out = [jnp.asarray(np_halves(t)) for t in moment_tables(node_values, c0, c1)]
     layers = 2 * cubes
     pairs = cubes // 2
     low_count = sum((pairs >> h) + 2 for h in range(cube_levels))
     top_count = sum((n // 2 >> h) + 2 for h in range(level_count - cube_levels))
-    halo_rows = 128 + 32 * cube_levels + 80
     f32, bf16 = jnp.float32, jnp.bfloat16
-    vmem = pl.BlockSpec(memory_space=pltpu.VMEM)
-    anywhere = pl.BlockSpec(memory_space=pl.ANY)
+    tables = (leaf_up, box_up, leaf_down, box_down, far, leaf_far, moment_in, moment_out)
+    stay = pl.BlockSpec(memory_space=pltpu.HBM)
     return pl.pallas_call(
         functools.partial(kernel_body, (nleaf, nsub, cubes, level_count), lengths, pieces),
         out_shape=jax.ShapeDtypeStruct(vectors.shape, f32),
-        in_specs=[vmem, vmem, pl.BlockSpec(memory_space=pltpu.SMEM), vmem, vmem, vmem,
-                  anywhere, vmem, anywhere, anywhere, vmem, vmem],
-        out_specs=vmem,
+        in_specs=[stay, stay, pl.BlockSpec(memory_space=pltpu.SMEM)] + [stay] * len(tables),
+        out_specs=pl.BlockSpec(memory_space=pltpu.VMEM),
         scratch_shapes=[
-            pltpu.VMEM((32, (layers + 2) * 256), bf16),
+            pltpu.VMEM(points.shape, f32),
+            pltpu.VMEM(vectors.shape, f32),
+            pltpu.VMEM((64, (layers + 2) * 256), bf16),
             pltpu.VMEM((8, (layers + 2) * 256), f32),
-            pltpu.VMEM((2, layers, 256, 256), bf16),
-            pltpu.VMEM((layers + 4, 32, 256), f32),
+            pltpu.VMEM((2, layers, 2, 128, 128), bf16),
+            pltpu.VMEM((128, layers * 256), bf16),
             pltpu.VMEM((layers + 4, 32, 256), bf16),
             pltpu.VMEM((layers + 4, 32, 256), bf16),
             pltpu.VMEM((2, 256, 512), f32),
             pltpu.VMEM((2, 256, 512), bf16),
             pltpu.VMEM((32, (layers + 2) * 256), f32),
-            pltpu.VMEM((2, halo_rows, 128), f32),
-            pltpu.VMEM((2, halo_rows, 128), f32),
-            pltpu.VMEM((16, 128), f32),
-            pltpu.VMEM((n, 16, 128), f32),
+            pltpu.VMEM((2, 208, 128), f32),
+            pltpu.VMEM((2, 208, 128), f32),
+            pltpu.VMEM((2, 32 * cube_levels, 128), f32),
+            pltpu.VMEM((2, 32 * cube_levels, 128), f32),
+            pltpu.VMEM((2, 8, 128), f32),
+            pltpu.VMEM((n, 8, 128), f32),
+            pltpu.VMEM((2, 16, 128), f32),
             pltpu.VMEM((low_count, 32, 128), f32),
-            pltpu.VMEM((top_count, 32, 128), f32),
-            pltpu.VMEM((8, 128), f32),
+            pltpu.VMEM((top_count, 16, 128), f32),
+            pltpu.VMEM((32, 256), bf16),
             pltpu.VMEM((layers, 32, 256), f32),
-            pltpu.VMEM(leaf_down.shape, bf16),
-            pltpu.VMEM(far.shape, bf16),
-            pltpu.VMEM(leaf_far.shape, bf16),
+        ] + [pltpu.VMEM(t.shape, bf16) for t in tables] + [
+            pltpu.SemaphoreType.DMA((6,)),
+            pltpu.SemaphoreType.DMA((6,)),
+            pltpu.SemaphoreType.DMA((1,)),
+            pltpu.SemaphoreType.DMA((1,)),
             pltpu.SemaphoreType.DMA((2,)),
-            pltpu.SemaphoreType.DMA((2,)),
-            pltpu.SemaphoreType.DMA((n,)),
-            pltpu.SemaphoreType.DMA((n,)),
-            pltpu.SemaphoreType.DMA((3,)),
+            pltpu.SemaphoreType.DMA((2 + len(tables),)),
         ],
         compiler_params=pltpu.CompilerParams(
-            collective_id=0, has_side_effects=True, vmem_limit_bytes=60 * 1024 * 1024
+            collective_id=0, has_side_effects=True, vmem_limit_bytes=VMEM_BYTES
         ),
-    )(points, vectors, counts, poly, leaf_up, box_up, leaf_down, box_down, far, leaf_far,
-      moment_in, moment_out)
+    )(points, vectors, counts, *tables)
 
 
 def solution(mesh):

time: 25 us -> 22.4 us (0.90)
  the two profiles are of different devices: /device:TPU:1 before, /device:TPU:0 now
where the time goes in v2:
time: 22.4 us; the launch traced here: 22.2 us
  Pallas kernels  20.3 us (91%)
  local copies, waits for them, and re-layouts  1.87 us (8%)
    pallas_call x1, Pallas kernels, local(): pl.pallas_call(functools.partial(kernel_body, (nleaf, nsub, cubes, level_...  20.3 us
    unnamed x1, local copies, waits for them, and re-layouts  1.87 us

profile of v2, /device:TPU:0, one launch (start us, length us, event | category | flops | bytes accessed | tf_op | source)
XLA Modules:
  0.0 22.2 jit_solution(5265421040294025416)
XLA Ops:
  0.0 20.3 %shard_map.109 = f32[32,4096]{1,0:T(8,128)} custom-call(f32[3,4096]{1,0:T(4,128)} %pts_hbm.1, f32[32,4096]{1,0:T(8,128)} %vec_hbm.1, s32[8,8]{1,0:T(8,128)} %cnt.1, bf16[2,1024,128]{2,1,0:T(8,128)(2,1)} %constant.16.clone.leaf_up_hbm, bf16[2,2,128,128]{3,2,1,0:T(8,128)(2,1)} %constant.18.clone.box_up_hbm, ...), custom_call_target="tpu_custom_call" | custom-call | tf_op jit(solution)/shard_map/pallas_call | solution.py:819
  20.4 1.9 %copy.13 = f32[32,4096]{1,0:T(8,128)} copy(f32[32,4096]{1,0:T(8,128)} %shard_map.109) | data formatting | bytes 1048576
